TPU v7x, 32 devices: a whole 2x2x4 slice. The times are simulated.
32 devices in a mesh: row: 4 (over z), col: 8 (over y, x, core).
Axes of the slice: x: 2, y: 2, z: 4, core: 2. Of those that a mesh axis runs over, the one named last changes fastest.
Arguments:
- slab: float32 [4096, 8192], P('row', 'col'), may hold values from -6 to 6
- owner: int32 [2], replicated, may hold values from 0 to 7, as said below
- leaf_reflectors: float32 [2, 4096, 2048], P(None, 'row', 'col'), may hold values from -0.1875 to 0.1875
- leaf_factors: float32 [2, 1024, 2048], P(None, 'row', 'col'), as said below
- tree_reflectors: float32 [2, 2, 1024, 256], P(None, None, 'row'), may hold values from -0.25 to 0.25
- tree_mixers: float32 [2, 2, 1024, 256], P(None, None, 'row'), may hold values from -0.1875 to 0.1875
Outputs:
- updated: float32 [4096, 8192], P('row', 'col')
Inputs may be any that keep to these rules, and one draw needn't show every extreme that they name: `owner`: the 2 owners are distinct column blocks, and one of them is the last column block. Every 256 x 256 block of leaf_factors is upper triangular with diagonal entries from 1 to 2.
All inputs are finite; a program needn't handle non-finite values.
Results may differ from a plain program's by a relative error of at most 0.00015.
Values sent between devices are 32-bit elements; how exact they have to be, the bound alone decides.
No kernel may reach another device: no remote copies, remote signals or barrier semaphores. Data moves between devices by JAX's collectives and lax.ppermute only.
A program may use at most 64 MiB of HBM per device.

v0:
```python
import jax
import jax.numpy as jnp
from jax import lax
from jax.sharding import PartitionSpec as P

HIGH = lax.Precision.HIGHEST
LEADING = (((0,), (0,)), ((), ()))


def from_partner(shard, axis, apart):
    return lax.ppermute(shard, axis, [(i, i ^ 1 << apart) for i in range(lax.axis_size(axis))])


def apply_leaf(matrix, received, first_row, rows_dev):
    reflect_rows = received[first_row:rows_dev]
    factor_block = received[rows_dev:]
    lower = matrix[first_row:]
    projected = lax.dot_general(
        reflect_rows, lower, LEADING, precision=HIGH, preferred_element_type=jnp.float32
    )
    scaled = lax.dot_general(
        factor_block, projected, LEADING, precision=HIGH, preferred_element_type=jnp.float32
    )
    lower = lower - jnp.dot(
        reflect_rows, scaled, precision=HIGH, preferred_element_type=jnp.float32
    )
    return jnp.concatenate([matrix[:first_row], lower], axis=0)


def tree_step(matrix, halves, mixers, first_row, width, levels):
    top_rows = matrix[first_row : first_row + width]
    for level_no in range(levels):
        partial_sum = lax.dot_general(
            halves[level_no], top_rows, LEADING, precision=HIGH, preferred_element_type=jnp.float32
        )
        partner_sum = from_partner(partial_sum, "row", level_no)
        top_rows = top_rows - jnp.dot(
            mixers[level_no],
            partial_sum + partner_sum,
            precision=HIGH,
            preferred_element_type=jnp.float32,
        )
    return lax.dynamic_update_slice_in_dim(matrix, top_rows, first_row, 0)


def shards(slab, owner, leaf_reflectors, leaf_factors, tree_reflectors, tree_mixers):
    rows_dev = slab.shape[0]
    width = leaf_factors.shape[1]
    panels = owner.shape[0]
    levels = lax.axis_size("row").bit_length() - 1
    is_owner = (lax.axis_index("col") == owner).astype(jnp.float32)
    stacked = jnp.concatenate([leaf_reflectors, leaf_factors], axis=1) * is_owner[:, None, None]
    received = lax.psum(stacked, "col")
    panel_blocks = [received[panel_no] for panel_no in range(panels)]
    matrix = slab
    for panel_no in range(panels):
        matrix = apply_leaf(matrix, panel_blocks[panel_no], panel_no * width, rows_dev)
        matrix = tree_step(
            matrix,
            tree_reflectors[panel_no],
            tree_mixers[panel_no],
            panel_no * width,
            width,
            levels,
        )
    return matrix


def solution(mesh):
    return jax.shard_map(
        shards,
        mesh=mesh,
        in_specs=(
            P("row", "col"),
            P(),
            P(None, "row", "col"),
            P(None, "row", "col"),
            P(None, None, "row", None),
            P(None, None, "row", None),
        ),
        out_specs=P("row", "col"),
        check_vma=False,
    )
```

profile of v0, /device:TPU:0, one launch (start us, length us, event | category | flops | bytes accessed | tf_op | source)
XLA Modules:
  0.0 220.8 jit_solution(15570357751311416546)
XLA Ops:
  6.5 0.0 all-reduce.2.cloned.1.call-start
  6.5 0.7 compare_convert_fusion
  7.2 3.5 %maximum_multiply_fusion = f32[2,1280,256]{2,1,0:T(8,128)} fusion(f32[2,256,256]{2,1,0:T(8,128)} %param.9, f32[2,1024,256]{2,1,0:T(8,128)} %param.8, f32[2]{0:T(128)S(1)} %compare_convert_fusion), kind=kLoop, calls=%fused_computation.4 | loop fusion | flops 1310720 | bytes 5242888 | tf_op jit(solution)/shard_map/mul | solution.py:52
  10.7 0.0 all-reduce.2.cloned.1.call-update
  10.7 67.5 %all-reduce.2.cloned.1.call-done = f32[2,1280,256]{2,1,0:T(8,128)} async-done(((f32[2,1280,256]{2,1,0:T(8,128)}), f32[2,1280,256]{2,1,0:T(8,128)}) %all-reduce.2.cloned.1.call-update) | async-done | bytes 2621456 | tf_op jit(solution)/shard_map/psum | solution.py:53
  78.2 0.0 copy-start
  78.2 0.0 copy-start.1
  78.2 6.2 %fusion.11 = f32[256,1024]{1,0:T(8,128)S(1)} fusion(f32[1024,1024]{1,0:T(8,128)} %param.6, f32[2,1280,256]{2,1,0:T(8,128)} %all-reduce.2.cloned.1.call-done), kind=kOutput, calls=%fused_computation.24 | convolution fusion | flops 3221225472 | bytes 6291456 | tf_op jit(solution)/shard_map/dot_general | solution.py:18
  84.4 2.0 fusion.15
  86.4 0.0 copy-done
  86.4 0.0 copy-done.1
  86.4 0.0 copy-start.2
  86.4 3.8 %convolution_subtract_fusion = f32[1024,1024]{1,0:T(8,128)S(1)} fusion(f32[1024,1024]{1,0:T(8,128)S(1)} %copy-done, f32[256,1024]{1,0:T(8,128)S(1)} %fusion.15, f32[2,1280,256]{2,1,0:T(8,128)S(1)} %copy-done.1), kind=kOutput, calls=%fused_computation.5 | convolution fusion | flops 3222274048 | bytes 10485760 | tf_op jit(solution)/shard_map/dot_general | solution.py:24
  90.2 0.0 copy-done.2
  90.2 1.9 convolution_bitcast_fusion.7
  92.1 1.6 collective-permute-start
  93.7 2.7 %fusion = f32[256,1024]{1,0:T(8,128)S(1)} fusion(f32[1024,1024]{1,0:T(8,128)S(1)} %convolution_subtract_fusion, f32[2,1280,256]{2,1,0:T(8,128)S(1)} %copy-done.1), kind=kOutput, calls=%fused_computation.2 | convolution fusion | flops 2415919104 | bytes 4980736 | tf_op jit(solution)/shard_map/dot_general | solution.py:18
  96.4 1.0 fusion.14
  97.4 0.0 copy-start.3
  97.5 3.0 %slice_subtract_fusion = f32[768,1024]{1,0:T(8,128)S(1)} fusion(f32[1024,1024]{1,0:T(8,128)S(1)} %convolution_subtract_fusion, f32[256,1024]{1,0:T(8,128)S(1)} %fusion.14, f32[2,1280,256]{2,1,0:T(8,128)S(1)} %copy-done.1), kind=kOutput, calls=%fused_computation.1 | convolution fusion | flops 2416705536 | bytes 8126464 | tf_op jit(solution)/shard_map/dot_general | solution.py:24
  100.5 1.8 convolution_bitcast_fusion.3
  102.3 0.6 collective-permute-start.2
  102.9 15.4 %collective-permute-done = f32[256,1024]{0,1:T(8,128)S(1)} collective-permute-done((f32[256,1024]{0,1:T(8,128)S(1)}, f32[256,1024]{0,1:T(8,128)S(1)}, u32[]{:S(2)}, u32[]{:S(2)}) %collective-permute-start) | collective-permute-done | bytes 1048608 | tf_op jit(solution)/shard_map/ppermute | solution.py:11
  118.3 0.0 copy-done.3
  118.3 1.2 fusion.2
  119.4 1.9 convolution_bitcast_fusion.5
  121.3 2.5 %collective-permute-start.1 = (f32[256,1024]{0,1:T(8,128)S(1)}, f32[256,1024]{0,1:T(8,128)S(1)}, u32[]{:S(2)}, u32[]{:S(2)}) collective-permute-start(f32[256,1024]{0,1:T(8,128)S(1)} %convolution_bitcast_fusion.5), channel_id=1, source_target_pairs={{0,16},{8,24},{16,0},{24,8},{1,17},{9,25},{17,1},{25,9},{2,18},{10... | collective-permute-start | bytes 3145736 | tf_op jit(solution)/shard_map/ppermute | solution.py:11
  123.8 34.6 %collective-permute-done.2 = f32[256,1024]{0,1:T(8,128)S(1)} collective-permute-done((f32[256,1024]{0,1:T(8,128)S(1)}, f32[256,1024]{0,1:T(8,128)S(1)}, u32[]{:S(2)}, u32[]{:S(2)}) %collective-permute-start.2) | collective-permute-done | bytes 1048608 | tf_op jit(solution)/shard_map/ppermute | solution.py:11
  158.4 1.1 fusion.4
  159.5 1.8 convolution_bitcast_fusion.1
  161.3 0.1 collective-permute-start.3
  161.4 31.2 %collective-permute-done.1 = f32[256,1024]{0,1:T(8,128)S(1)} collective-permute-done((f32[256,1024]{0,1:T(8,128)S(1)}, f32[256,1024]{0,1:T(8,128)S(1)}, u32[]{:S(2)}, u32[]{:S(2)}) %collective-permute-start.1) | collective-permute-done | bytes 1048608 | tf_op jit(solution)/shard_map/ppermute | solution.py:11
  192.6 1.2 fusion.3
  193.8 2.6 %pad_maximum_fusion = f32[1024,1024]{1,0:T(8,128)} fusion(f32[768,1024]{1,0:T(8,128)S(1)} %slice_subtract_fusion, f32[256,1024]{1,0:T(8,128)S(1)} %fusion.3), kind=kLoop, calls=%fused_computation | loop fusion | flops 1048576 | bytes 8388608 | tf_op jit(solution)/shard_map/concatenate | solution.py:27
  196.4 15.4 %collective-permute-done.3 = f32[256,1024]{0,1:T(8,128)S(1)} collective-permute-done((f32[256,1024]{0,1:T(8,128)S(1)}, f32[256,1024]{0,1:T(8,128)S(1)}, u32[]{:S(2)}, u32[]{:S(2)}) %collective-permute-start.3) | collective-permute-done | bytes 1048608 | tf_op jit(solution)/shard_map/ppermute | solution.py:11
  211.9 2.1 fusion.6
Async XLA Ops:
  6.5 71.7 %all-reduce.2.cloned.1.call-start = ((), (), s32[]{:S(2)}) async-start(), calls=%async_computation | async-start | bytes 5242880 | tf_op jit(solution)/shard_map/psum | solution.py:53
  78.2 8.2 %copy-start = (f32[1024,1024]{1,0:T(8,128)S(1)}, f32[1024,1024]{1,0:T(8,128)}, u32[]{:S(2)}) copy-start(f32[1024,1024]{1,0:T(8,128)} %param.6) | copy-start | bytes 12582916
  78.2 8.2 %copy-start.1 = (f32[2,1280,256]{2,1,0:T(8,128)S(1)}, f32[2,1280,256]{2,1,0:T(8,128)}, u32[]{:S(2)}) copy-start(f32[2,1280,256]{2,1,0:T(8,128)} %all-reduce.2.cloned.1.call-done) | copy-start | bytes 7864324
  86.4 3.8 %copy-start.2 = (f32[2,2,256,256]{3,2,1,0:T(8,128)S(1)}, f32[2,2,256,256]{3,2,1,0:T(8,128)}, u32[]{:S(2)}) copy-start(f32[2,2,256,256]{3,2,1,0:T(8,128)} %param.10) | copy-start | bytes 3145732
  92.1 26.2 %collective-permute-start = (f32[256,1024]{0,1:T(8,128)S(1)}, f32[256,1024]{0,1:T(8,128)S(1)}, u32[]{:S(2)}, u32[]{:S(2)}) collective-permute-start(f32[256,1024]{0,1:T(8,128)S(1)} %convolution_bitcast_fusion.7), channel_id=1, source_target_pairs={{0,8},{8,0},{16,24},{24,16},{1,9},{9,1},{17,25},{25,17},{2,10},{10... | collective-permute-start | bytes 3145736 | tf_op jit(solution)/shard_map/ppermute | solution.py:11
  97.4 20.8 %copy-start.3 = (f32[2,2,256,256]{3,2,1,0:T(8,128)S(1)}, f32[2,2,256,256]{3,2,1,0:T(8,128)}, u32[]{:S(2)}) copy-start(f32[2,2,256,256]{3,2,1,0:T(8,128)} %param.11) | copy-start | bytes 3145732
  102.3 56.1 %collective-permute-start.2 = (f32[256,1024]{0,1:T(8,128)S(1)}, f32[256,1024]{0,1:T(8,128)S(1)}, u32[]{:S(2)}, u32[]{:S(2)}) collective-permute-start(f32[256,1024]{0,1:T(8,128)S(1)} %convolution_bitcast_fusion.3), channel_id=1, source_target_pairs={{0,8},{8,0},{16,24},{24,16},{1,9},{9,1},{17,25},{25,17},{2,10},{10... | collective-permute-start | bytes 3145736 | tf_op jit(solution)/shard_map/ppermute | solution.py:11
  121.3 71.3 %collective-permute-start.1 = (f32[256,1024]{0,1:T(8,128)S(1)}, f32[256,1024]{0,1:T(8,128)S(1)}, u32[]{:S(2)}, u32[]{:S(2)}) collective-permute-start(f32[256,1024]{0,1:T(8,128)S(1)} %convolution_bitcast_fusion.5), channel_id=1, source_target_pairs={{0,16},{8,24},{16,0},{24,8},{1,17},{9,25},{17,1},{25,9},{2,18},{10... | collective-permute-start | bytes 3145736 | tf_op jit(solution)/shard_map/ppermute | solution.py:11
  161.3 50.5 %collective-permute-start.3 = (f32[256,1024]{0,1:T(8,128)S(1)}, f32[256,1024]{0,1:T(8,128)S(1)}, u32[]{:S(2)}, u32[]{:S(2)}) collective-permute-start(f32[256,1024]{0,1:T(8,128)S(1)} %convolution_bitcast_fusion.1), channel_id=1, source_target_pairs={{0,16},{8,24},{16,0},{24,8},{1,17},{9,25},{17,1},{25,9},{2,18},{10... | collective-permute-start | bytes 3145736 | tf_op jit(solution)/shard_map/ppermute | solution.py:11
Sparse Core Ops, SparseCore 0:
  10.8 67.3 all-reduce.1
where the time goes:
time: 221 us
  waiting for transfers between devices  164 us (74%)
  matrix products  31.7 us (14%)
  between operations  13.5 us (6%)
  other arithmetic  6.76 us (3%)
  starting transfers between devices  4.7 us (2%)
    ppermute x4, waiting for transfers between devices, from_partner(): lax.ppermute(shard, axis, [(i, i ^ 1 << apart) for i in range(lax.axis_si...  96.6 us
    psum x1, waiting for transfers between devices, shards(): received = lax.psum(stacked, 'col')  67.5 us
    dot_general x2, matrix products, apply_leaf(): lax.dot_general(reflect_rows, lower, LEADING, precision=HIGH, preferred_e...  8.91 us
    dot_general x4, matrix products, tree_step(): lax.dot_general(halves[level_no], top_rows, LEADING, precision=HIGH, pref...  7.35 us
    dot_general x2, matrix products, apply_leaf(): jnp.dot(reflect_rows, scaled, precision=HIGH, preferred_element_type=jnp....  6.81 us
    dot_general x4, matrix products, tree_step(): jnp.dot(mixers[level_no], partial_sum + partner_sum, precision=HIGH, pref...  5.55 us
    ppermute x4, starting transfers between devices, from_partner(): lax.ppermute(shard, axis, [(i, i ^ 1 << apart) for i in range(lax.axis_si...  4.69 us
  transfers between devices with their start and end apart: 5, of which 5 were waited for; matrix products, arithmetic and copies ran while one was open for 8% of the time, Pallas kernels for 0%

commit v1 on v0

--- a/solution.py
+++ b/solution.py
@@ -50,7 +50,9 @@
     levels = lax.axis_size("row").bit_length() - 1
     is_owner = (lax.axis_index("col") == owner).astype(jnp.float32)
     stacked = jnp.concatenate([leaf_reflectors, leaf_factors], axis=1) * is_owner[:, None, None]
-    received = lax.psum(stacked, "col")
+    received = stacked
+    for hop in (1, 2, 4):
+        received = received + lax.ppermute(received, "col", [(dev, dev ^ hop) for dev in range(8)])
     panel_blocks = [received[panel_no] for panel_no in range(panels)]
     matrix = slab
     for panel_no in range(panels):

time: 221 us -> 262 us (1.19)
  waiting for transfers between devices: 164 us -> 217 us
  between operations: 13.5 us -> 0.17 us
  starting transfers between devices: 4.7 us -> 10.1 us
  matrix products: 31.7 us -> 28.4 us
    ppermute x0 -> x3, waiting for transfers between devices: none -> 118 us  [shards(): lax.ppermute(received, 'col', [(dev, dev ^ hop) for dev in range(8)])]
    psum x1 -> x0, waiting for transfers between devices: 67.5 us -> none  [shards(): received = lax.psum(stacked, 'col')]
    ppermute x0 -> x3, starting transfers between devices: none -> 5.28 us  [shards(): lax.ppermute(received, 'col', [(dev, dev ^ hop) for dev in range(8)])]
  transfers between devices with their start and end apart: 5 -> 7, of which waited for: 5 -> 7; matrix products, arithmetic and copies ran while one was open for 8% -> 6% of each run, Pallas kernels for 0% -> 0%
where the time goes in v1:
time: 262 us
  waiting for transfers between devices  217 us (83%)
  matrix products  28.4 us (11%)
  starting transfers between devices  10.1 us (4%)
  other arithmetic  6.28 us (2%)
    ppermute x3, waiting for transfers between devices, shards(): lax.ppermute(received, 'col', [(dev, dev ^ hop) for dev in range(8)])  118 us
    ppermute x4, waiting for transfers between devices, from_partner(): lax.ppermute(shard, axis, [(i, i ^ 1 << apart) for i in range(lax.axis_si...  98.8 us
    dot_general x4, matrix products, tree_step(): lax.dot_general(halves[level_no], top_rows, LEADING, precision=HIGH, pref...  7.57 us
    dot_general x2, matrix products, apply_leaf(): lax.dot_general(reflect_rows, lower, LEADING, precision=HIGH, preferred_e...  6.62 us
    dot_general x2, matrix products, apply_leaf(): jnp.dot(reflect_rows, scaled, precision=HIGH, preferred_element_type=jnp....  6.56 us
    dot_general x4, matrix products, tree_step(): jnp.dot(mixers[level_no], partial_sum + partner_sum, precision=HIGH, pref...  5.55 us
    ppermute x3, starting transfers between devices, shards(): lax.ppermute(received, 'col', [(dev, dev ^ hop) for dev in range(8)])  5.28 us
  transfers between devices with their start and end apart: 7, of which 7 were waited for; matrix products, arithmetic and copies ran while one was open for 6% of the time, Pallas kernels for 0%

profile of v1, /device:TPU:0, one launch (start us, length us, event | category | flops | bytes accessed | tf_op | source)
XLA Modules:
  0.0 262.0 jit_solution(15208589050875021806)
XLA Ops:
  0.0 0.7 compare_convert_fusion
  0.7 2.0 maximum_multiply_fusion
  2.7 0.5 collective-permute-start
  3.2 4.5 %collective-permute-done = f32[2,1280,256]{2,1,0:T(8,128)S(1)} collective-permute-done((f32[2,1280,256]{2,1,0:T(8,128)S(1)}, f32[2,1280,256]{2,1,0:T(8,128)S(1)}, u32[]{:S(2)}, u32[]{:S(2)}) %collective-permute-start) | collective-permute-done | bytes 2621472 | tf_op jit(solution)/shard_map/ppermute | solution.py:55
  7.7 0.3 add.21
  8.1 2.9 %collective-permute-start.1 = (f32[2,1280,256]{2,1,0:T(8,128)S(1)}, f32[2,1280,256]{2,1,0:T(8,128)S(1)}, u32[]{:S(2)}, u32[]{:S(2)}) collective-permute-start(f32[2,1280,256]{2,1,0:T(8,128)S(1)} %add.21), channel_id=1, source_target_pairs={{0,2},{1,3},{2,0},{3,1},{4,6},{5,7},{6,4},{7,5},{8,10},{9,11},{10,... | collective-permute-start | bytes 7864328 | tf_op jit(solution)/shard_map/ppermute | solution.py:55
  11.0 57.2 %collective-permute-done.1 = f32[2,1280,256]{2,1,0:T(8,128)S(1)} collective-permute-done((f32[2,1280,256]{2,1,0:T(8,128)S(1)}, f32[2,1280,256]{2,1,0:T(8,128)S(1)}, u32[]{:S(2)}, u32[]{:S(2)}) %collective-permute-start.1) | collective-permute-done | bytes 2621472 | tf_op jit(solution)/shard_map/ppermute | solution.py:55
  68.2 0.3 add.22
  68.5 0.0 copy-start
  68.5 1.8 collective-permute-start.2
  70.3 56.6 %collective-permute-done.2 = f32[2,1280,256]{2,1,0:T(8,128)S(1)} collective-permute-done((f32[2,1280,256]{2,1,0:T(8,128)S(1)}, f32[2,1280,256]{2,1,0:T(8,128)S(1)}, u32[]{:S(2)}, u32[]{:S(2)}) %collective-permute-start.2) | collective-permute-done | bytes 2621472 | tf_op jit(solution)/shard_map/ppermute | solution.py:55
  127.0 0.3 add.23
  127.3 0.0 copy-done
  127.3 3.7 %fusion.11 = f32[256,1024]{1,0:T(8,128)S(1)} fusion(f32[1024,1024]{1,0:T(8,128)S(1)} %copy-done, f32[2,1280,256]{2,1,0:T(8,128)S(1)} %add.23), kind=kOutput, calls=%fused_computation.24 | convolution fusion | flops 3221225472 | bytes 6291456 | tf_op jit(solution)/shard_map/dot_general | solution.py:18
  131.0 1.0 fusion.15
  132.1 3.8 %convolution_subtract_fusion = f32[1024,1024]{1,0:T(8,128)S(1)} fusion(f32[1024,1024]{1,0:T(8,128)S(1)} %copy-done, f32[256,1024]{1,0:T(8,128)S(1)} %fusion.15, f32[2,1280,256]{2,1,0:T(8,128)S(1)} %add.23), kind=kOutput, calls=%fused_computation.5 | convolution fusion | flops 3222274048 | bytes 10485760 | tf_op jit(solution)/shard_map/dot_general | solution.py:24
  135.9 0.0 copy-start.1
  135.9 2.9 %fusion = f32[256,1024]{1,0:T(8,128)S(1)} fusion(f32[1024,1024]{1,0:T(8,128)S(1)} %convolution_subtract_fusion, f32[2,1280,256]{2,1,0:T(8,128)S(1)} %add.23), kind=kOutput, calls=%fused_computation.2 | convolution fusion | flops 2415919104 | bytes 4980736 | tf_op jit(solution)/shard_map/dot_general | solution.py:18
  138.8 1.0 fusion.14
  139.9 0.0 copy-done.1
  139.9 1.9 convolution_bitcast_fusion.7
  141.7 0.0 copy-start.2
  141.8 1.6 collective-permute-start.3
  143.3 2.8 %slice_subtract_fusion = f32[768,1024]{1,0:T(8,128)S(1)} fusion(f32[1024,1024]{1,0:T(8,128)S(1)} %convolution_subtract_fusion, f32[256,1024]{1,0:T(8,128)S(1)} %fusion.14, f32[2,1280,256]{2,1,0:T(8,128)S(1)} %add.23), kind=kOutput, calls=%fused_computation.1 | convolution fusion | flops 2416705536 | bytes 8126464 | tf_op jit(solution)/shard_map/dot_general | solution.py:24
  146.1 1.8 convolution_bitcast_fusion.3
  147.9 0.6 collective-permute-start.5
  148.5 19.4 %collective-permute-done.3 = f32[256,1024]{0,1:T(8,128)S(1)} collective-permute-done((f32[256,1024]{0,1:T(8,128)S(1)}, f32[256,1024]{0,1:T(8,128)S(1)}, u32[]{:S(2)}, u32[]{:S(2)}) %collective-permute-start.3) | collective-permute-done | bytes 1048608 | tf_op jit(solution)/shard_map/ppermute | solution.py:11
  167.9 0.0 copy-done.2
  167.9 1.2 fusion.2
  169.1 1.9 convolution_bitcast_fusion.5
  171.0 2.6 collective-permute-start.4
  173.5 34.3 %collective-permute-done.5 = f32[256,1024]{0,1:T(8,128)S(1)} collective-permute-done((f32[256,1024]{0,1:T(8,128)S(1)}, f32[256,1024]{0,1:T(8,128)S(1)}, u32[]{:S(2)}, u32[]{:S(2)}) %collective-permute-start.5) | collective-permute-done | bytes 1048608 | tf_op jit(solution)/shard_map/ppermute | solution.py:11
  207.8 1.1 fusion.4
  209.0 2.0 convolution_bitcast_fusion.1
  211.0 0.1 collective-permute-start.6
  211.1 29.0 %collective-permute-done.4 = f32[256,1024]{0,1:T(8,128)S(1)} collective-permute-done((f32[256,1024]{0,1:T(8,128)S(1)}, f32[256,1024]{0,1:T(8,128)S(1)}, u32[]{:S(2)}, u32[]{:S(2)}) %collective-permute-start.4) | collective-permute-done | bytes 1048608 | tf_op jit(solution)/shard_map/ppermute | solution.py:11
  240.1 1.2 fusion.3
  241.3 2.6 pad_maximum_fusion
  243.9 16.0 %collective-permute-done.6 = f32[256,1024]{0,1:T(8,128)S(1)} collective-permute-done((f32[256,1024]{0,1:T(8,128)S(1)}, f32[256,1024]{0,1:T(8,128)S(1)}, u32[]{:S(2)}, u32[]{:S(2)}) %collective-permute-start.6) | collective-permute-done | bytes 1048608 | tf_op jit(solution)/shard_map/ppermute | solution.py:11
  260.0 2.1 fusion.6
Async XLA Ops:
  2.7 5.1 %collective-permute-start = (f32[2,1280,256]{2,1,0:T(8,128)S(1)}, f32[2,1280,256]{2,1,0:T(8,128)S(1)}, u32[]{:S(2)}, u32[]{:S(2)}) collective-permute-start(f32[2,1280,256]{2,1,0:T(8,128)S(1)} %maximum_multiply_fusion), channel_id=1, source_target_pairs={{0,1},{1,0},{2,3},{3,2},{4,5},{5,4},{6,7},{7,6},{8,9},{9,8},{10,11... | collective-permute-start | bytes 7864328 | tf_op jit(solution)/shard_map/ppermute | solution.py:55
  8.1 60.1 %collective-permute-start.1 = (f32[2,1280,256]{2,1,0:T(8,128)S(1)}, f32[2,1280,256]{2,1,0:T(8,128)S(1)}, u32[]{:S(2)}, u32[]{:S(2)}) collective-permute-start(f32[2,1280,256]{2,1,0:T(8,128)S(1)} %add.21), channel_id=1, source_target_pairs={{0,2},{1,3},{2,0},{3,1},{4,6},{5,7},{6,4},{7,5},{8,10},{9,11},{10,... | collective-permute-start | bytes 7864328 | tf_op jit(solution)/shard_map/ppermute | solution.py:55
  68.5 58.8 %copy-start = (f32[1024,1024]{1,0:T(8,128)S(1)}, f32[1024,1024]{1,0:T(8,128)}, u32[]{:S(2)}) copy-start(f32[1024,1024]{1,0:T(8,128)} %param.6) | copy-start | bytes 12582916
  68.5 58.5 %collective-permute-start.2 = (f32[2,1280,256]{2,1,0:T(8,128)S(1)}, f32[2,1280,256]{2,1,0:T(8,128)S(1)}, u32[]{:S(2)}, u32[]{:S(2)}) collective-permute-start(f32[2,1280,256]{2,1,0:T(8,128)S(1)} %add.22), channel_id=1, source_target_pairs={{0,4},{1,5},{2,6},{3,7},{4,0},{5,1},{6,2},{7,3},{8,12},{9,13},{10,... | collective-permute-start | bytes 7864328 | tf_op jit(solution)/shard_map/ppermute | solution.py:55
  135.9 4.0 %copy-start.1 = (f32[2,2,256,256]{3,2,1,0:T(8,128)S(1)}, f32[2,2,256,256]{3,2,1,0:T(8,128)}, u32[]{:S(2)}) copy-start(f32[2,2,256,256]{3,2,1,0:T(8,128)} %param.10) | copy-start | bytes 3145732
  141.7 26.2 %copy-start.2 = (f32[2,2,256,256]{3,2,1,0:T(8,128)S(1)}, f32[2,2,256,256]{3,2,1,0:T(8,128)}, u32[]{:S(2)}) copy-start(f32[2,2,256,256]{3,2,1,0:T(8,128)} %param.11) | copy-start | bytes 3145732
  141.8 26.2 %collective-permute-start.3 = (f32[256,1024]{0,1:T(8,128)S(1)}, f32[256,1024]{0,1:T(8,128)S(1)}, u32[]{:S(2)}, u32[]{:S(2)}) collective-permute-start(f32[256,1024]{0,1:T(8,128)S(1)} %convolution_bitcast_fusion.7), channel_id=1, source_target_pairs={{0,8},{8,0},{16,24},{24,16},{1,9},{9,1},{17,25},{25,17},{2,10},{10... | collective-permute-start | bytes 3145736 | tf_op jit(solution)/shard_map/ppermute | solution.py:11
  147.9 59.9 %collective-permute-start.5 = (f32[256,1024]{0,1:T(8,128)S(1)}, f32[256,1024]{0,1:T(8,128)S(1)}, u32[]{:S(2)}, u32[]{:S(2)}) collective-permute-start(f32[256,1024]{0,1:T(8,128)S(1)} %convolution_bitcast_fusion.3), channel_id=1, source_target_pairs={{0,8},{8,0},{16,24},{24,16},{1,9},{9,1},{17,25},{25,17},{2,10},{10... | collective-permute-start | bytes 3145736 | tf_op jit(solution)/shard_map/ppermute | solution.py:11
  171.0 69.2 %collective-permute-start.4 = (f32[256,1024]{0,1:T(8,128)S(1)}, f32[256,1024]{0,1:T(8,128)S(1)}, u32[]{:S(2)}, u32[]{:S(2)}) collective-permute-start(f32[256,1024]{0,1:T(8,128)S(1)} %convolution_bitcast_fusion.5), channel_id=1, source_target_pairs={{0,16},{8,24},{16,0},{24,8},{1,17},{9,25},{17,1},{25,9},{2,18},{10... | collective-permute-start | bytes 3145736 | tf_op jit(solution)/shard_map/ppermute | solution.py:11
  211.0 48.9 %collective-permute-start.6 = (f32[256,1024]{0,1:T(8,128)S(1)}, f32[256,1024]{0,1:T(8,128)S(1)}, u32[]{:S(2)}, u32[]{:S(2)}) collective-permute-start(f32[256,1024]{0,1:T(8,128)S(1)} %convolution_bitcast_fusion.1), channel_id=1, source_target_pairs={{0,16},{8,24},{16,0},{24,8},{1,17},{9,25},{17,1},{25,9},{2,18},{10... | collective-permute-start | bytes 3145736 | tf_op jit(solution)/shard_map/ppermute | solution.py:11
